TPU v7x, 32 devices: a whole 2x2x4 slice. The times are simulated.
32 devices in a mesh: expert: 4 (over z), dp: 8 (over y, x, core).
Axes of the slice: x: 2, y: 2, z: 4, core: 2. Of those that a mesh axis runs over, the one named last changes fastest.
Arguments:
- row_acts: bfloat16 [4, 8192, 2048], P('expert', 'dp'), may hold values from -6 to 6
- row_grads: bfloat16 [4, 8192, 768], P('expert', 'dp'), may hold values from -6 to 6
- grad_factor: bfloat16 [4, 768, 768], P('expert', None, 'dp'), may hold values from -0.21875 to 0.21875
- value_factor: bfloat16 [4, 2048, 768], P('expert', None, 'dp'), may hold values from -0.125 to 0.125
- counts: int32 [4, 8], P('expert', 'dp'), may hold values from 128 to 1024, as said below
- row_token: int32 [4, 8192], P('expert', 'dp'), may hold values from 0 to 1023, as said below
Outputs:
- influence: float32 [8192, 24], P(('expert', 'dp'))
Inputs may be any that keep to these rules, and one draw needn't show every extreme that they name: counts[e, b] slots at the start of each block of 1024 slots are live; some block has all 1024 live. `row_token`: within one block of 1024 slots of one expert the ids are distinct, dead slots included.
All inputs are finite; a program needn't handle non-finite values.
Results may differ from a plain program's by a relative error of at most 0.0003.
Values may be sent and summed in bfloat16 or wider, within the bound.
A program may use at most 64 MiB of HBM per device.

v0:
```python
import jax
import jax.numpy as jnp
from jax import lax
from jax.sharding import PartitionSpec as P

MODEL = 2048
MOE_FF = 768
RANK = 32
QUERIES = 24
TOK_DEV = 256


epsilon = 1e-06


def local(row_acts, row_grads, grad_factor, value_factor, counts, row_token):
    activ = row_acts[0]
    gradient = row_grads[0]
    acts_proj = jnp.dot(
        activ,
        lax.all_gather(value_factor[0], "dp", axis=1, tiled=True),
        preferred_element_type=jnp.float32,
    )
    grads_proj = jnp.dot(
        gradient,
        lax.all_gather(grad_factor[0], "dp", axis=1, tiled=True),
        preferred_element_type=jnp.float32,
    )
    columns_all = acts_proj.shape[1]
    column_ids = lax.broadcasted_iota(jnp.int32, (columns_all, QUERIES), 0) // RANK
    query_ids = lax.broadcasted_iota(jnp.int32, (columns_all, QUERIES), 1)
    grouping = (column_ids == query_ids).astype(jnp.float32)
    scores = jnp.dot(acts_proj * grads_proj, grouping, precision=lax.Precision.HIGHEST)
    slots = activ.shape[0]
    live = lax.broadcasted_iota(jnp.int32, (slots,), 0) < counts[0, 0]
    norms = jnp.sum(jnp.square(activ.astype(jnp.float32)), 1) * jnp.sum(
        jnp.square(gradient.astype(jnp.float32)), 1
    )
    shard_tokens = TOK_DEV * lax.axis_size("expert")
    owner_grid = lax.broadcasted_iota(jnp.int32, (slots, shard_tokens), 1)
    onehot = ((row_token[0][:, None] == owner_grid) & live[:, None]).astype(jnp.float32)
    contract = (((0,), (0,)), ((), ()))
    dense = lax.dot_general(onehot, scores, contract, precision=lax.Precision.HIGHEST)
    dense_norm = lax.dot_general(onehot, norms[:, None], contract, precision=lax.Precision.HIGHEST)[
        :, 0
    ]
    totals, norm_sum = (
        lax.psum_scatter(dense, "expert", scatter_dimension=0, tiled=True),
        lax.psum_scatter(dense_norm, "expert", scatter_dimension=0, tiled=True),
    )
    factor = lax.rsqrt(norm_sum / (MODEL * MOE_FF) + epsilon) / jnp.sqrt(jnp.float32(RANK))
    return totals * factor[:, None]


def solution(mesh):
    return jax.shard_map(
        local,
        mesh=mesh,
        in_specs=(
            P("expert", "dp", None),
            P("expert", "dp", None),
            P("expert", None, "dp"),
            P("expert", None, "dp"),
            P("expert", "dp"),
            P("expert", "dp"),
        ),
        out_specs=P(("expert", "dp"), None),
        check_vma=False,
    )
```

profile of v0, /device:TPU:0, one launch (start us, length us, event | category | flops | bytes accessed | tf_op | source)
XLA Modules:
  0.0 107.9 jit_solution(8204518009770118242)
XLA Ops:
  6.5 0.0 all-gather.7.cloned.1.call-start
  6.5 0.7 all-gather.7.cloned.1.call-update
  7.3 0.0 all-gather.5.cloned.1.call-start
  7.3 0.7 all-gather.5.cloned.1.call-update
  8.0 0.0 reduce-scatter.2.cloned.1.call-start
  8.7 1.8 %multiply_reduce_fusion.1 = f32[1024]{0:T(1024)S(1)} fusion(bf16[1,1024,768]{2,1,0:T(8,128)(2,1)} %param.7), kind=kLoop, calls=%fused_computation.8 | loop fusion | flops 2358272 | bytes 1576960 | tf_op jit(solution)/shard_map/reduce_sum | solution.py:36
  10.5 3.1 %multiply_reduce_fusion = f32[1024]{0:T(1024)S(1)} fusion(bf16[1,1024,2048]{2,1,0:T(8,128)(2,1)} %param.6), kind=kLoop, calls=%fused_computation | loop fusion | flops 6290432 | bytes 4198400 | tf_op jit(solution)/shard_map/reduce_sum | solution.py:36
  13.6 22.3 %all-gather.7.cloned.1.call-done = bf16[1,768,768]{1,2,0:T(8,128)(2,1)} async-done(((bf16[1,768,96]{1,2,0:T(8,128)(2,1)}), bf16[1,768,768]{1,2,0:T(8,128)(2,1)}) %all-gather.7.cloned.1.call-update) | async-done | bytes 1179664 | tf_op jit(solution)/shard_map/all_gather | solution.py:26
  35.9 3.2 %fusion.14 = f32[1024,768]{1,0:T(8,128)S(1)} fusion(bf16[1,1024,768]{2,1,0:T(8,128)(2,1)} %param.7, bf16[1,768,768]{1,2,0:T(8,128)(2,1)} %all-gather.7.cloned.1.call-done), kind=kOutput, calls=%fused_computation.15 | convolution fusion | flops 1207959552 | bytes 5898240 | tf_op jit(solution)/shard_map/dot_general | solution.py:24
  39.1 30.9 %all-gather.5.cloned.1.call-done = bf16[1,2048,768]{1,2,0:T(8,128)(2,1)} async-done(((bf16[1,2048,96]{1,2,0:T(8,128)(2,1)}), bf16[1,2048,768]{1,2,0:T(8,128)(2,1)}) %all-gather.5.cloned.1.call-update) | async-done | bytes 3145744 | tf_op jit(solution)/shard_map/all_gather | solution.py:21
  70.0 6.2 %fusion = f32[1024,768]{1,0:T(8,128)S(1)} fusion(bf16[1,1024,2048]{2,1,0:T(8,128)(2,1)} %param.6, bf16[1,2048,768]{1,2,0:T(8,128)(2,1)} %all-gather.5.cloned.1.call-done), kind=kOutput, calls=%fused_computation.1 | convolution fusion | flops 3221225472 | bytes 10485760 | tf_op jit(solution)/shard_map/dot_general | solution.py:19
  76.2 0.0 copy-start
  76.2 1.8 %fusion.8 = f32[1024,24]{1,0:T(8,128)S(1)} fusion(f32[1024,768]{1,0:T(8,128)S(1)} %fusion, f32[1024,768]{1,0:T(8,128)S(1)} %fusion.14, s32[768]{0:T(1024)S(1)} %get-tuple-element.5, s32[768]{0:T(1024)S(1)} %get-tuple-element.6, pred[768]{0:T(1024)(128)(4,1)S(1)} %fusion.22), kind=kOutput, calls=%fused_computation.9 | convolution fusion | flops 227315712 | bytes 6396672 | tf_op jit(solution)/shard_map/dot_general | solution.py:33
  78.0 0.0 copy-start.1
  78.1 0.0 copy-done
  78.1 2.4 %fusion.5 = f32[1024,24]{0,1:T(8,128)} fusion(f32[1024,24]{1,0:T(8,128)S(1)} %fusion.8, s32[1024]{0:T(1024)S(1)} %bitcast.24, pred[1024]{0:T(1024)(128)(4,1)S(1)} %iota_compare_fusion.3), kind=kOutput, calls=%fused_computation.6 | convolution fusion | flops 304087040 | bytes 201728 | tf_op jit(solution)/shard_map/dot_general | solution.py:43
  80.4 0.0 reduce-scatter.2.cloned.1.call-update
  80.5 1.6 %fusion.3 = f32[1,1024]{1,0:T(1,128)S(1)} fusion(f32[1024,1]{0,1:T(1,128)S(1)} %bitcast.22, s32[1024]{0:T(1024)S(1)} %bitcast.25, pred[1024]{0:T(1024)(128)(4,1)S(1)} %iota_compare_fusion.3), kind=kOutput, calls=%fused_computation.5 | convolution fusion | flops 14680064 | bytes 13312 | tf_op jit(solution)/shard_map/dot_general | solution.py:44
  82.0 0.0 copy-done.1
  82.0 0.6 dynamic-slice
  83.3 11.7 %all-reduce = f32[1024]{0:T(1024)S(1)} all-reduce(f32[1024]{0:T(1024)S(1)} %bitcast.23), channel_id=5, replica_groups=mesh['expert'=4,'dp'=8] {'expert'}, use_global_device_ids=true, to_apply=%region_3.4.clone | all-reduce | flops 1024 | bytes 8192
  95.0 0.1 fusion.25
  95.1 4.9 %reduce-scatter.2.cloned.1.call-done = f32[256,24]{0,1:T(8,128)} async-done(((f32[1024,24]{0,1:T(8,128)}), f32[256,24]{0,1:T(8,128)}) %reduce-scatter.2.cloned.1.call-update) | async-done | bytes 24592 | tf_op jit(solution)/shard_map/reduce_scatter | solution.py:48
  100.0 1.3 %broadcast_multiply_fusion = f32[256,24]{0,1:T(8,128)} fusion(f32[256,24]{0,1:T(8,128)} %reduce-scatter.2.cloned.1.call-done, f32[256]{0:T(256)S(1)} %fusion.25), kind=kLoop, calls=%fused_computation.22 | loop fusion | flops 6144 | bytes 50176 | tf_op jit(solution)/shard_map/mul | solution.py:52
  (4 shorter events, 0.0 us)
Async XLA Ops:
  6.5 29.4 %all-gather.7.cloned.1.call-start = ((), (), s32[]{:S(2)}) async-start(), calls=%async_computation.3 | async-start | bytes 1327104 | tf_op jit(solution)/shard_map/all_gather | solution.py:26
  7.3 62.7 %all-gather.5.cloned.1.call-start = ((), (), s32[]{:S(2)}) async-start(), calls=%async_computation.2 | async-start | bytes 3538944 | tf_op jit(solution)/shard_map/all_gather | solution.py:21
  8.0 92.0 %reduce-scatter.2.cloned.1.call-start = ((), (), s32[]{:S(2)}) async-start(), calls=%async_computation.1 | async-start | bytes 122880 | tf_op jit(solution)/shard_map/reduce_scatter | solution.py:48
  76.2 1.9 %copy-start = (s32[1,1024]{1,0:T(1,128)S(1)}, s32[1,1024]{1,0:T(1,128)}, u32[]{:S(2)}) copy-start(s32[1,1024]{1,0:T(1,128)} %param.11) | copy-start | bytes 12292
  78.0 4.0 %copy-start.1 = (u32[32]{0:T(128)S(1)}, u32[32]{0:T(128)}, u32[]{:S(2)}) copy-start(u32[32]{0:T(128)} %constant.38) | copy-start | bytes 388
Sparse Core Ops, SparseCore 0:
  9.2 26.6 all-gather.6
  37.8 32.1 all-gather.4
  80.6 19.3 reduce-scatter.1
where the time goes:
time: 108 us
  waiting for transfers between devices  59.5 us (55%)
  matrix products  15.1 us (14%)
  between operations  14.5 us (13%)
  blocking collectives  11.7 us (11%)
  other arithmetic  6.31 us (6%)
    all_gather x1, waiting for transfers between devices, local(): lax.all_gather(value_factor[0], 'dp', axis=1, tiled=True)  30.9 us
    all_gather x1, waiting for transfers between devices, local(): lax.all_gather(grad_factor[0], 'dp', axis=1, tiled=True)  22.3 us
    unnamed x1, blocking collectives  11.7 us
    dot_general x1, matrix products, local(): jnp.dot(activ, lax.all_gather(value_factor[0], 'dp', axis=1, tiled=True),...  6.22 us
    reduce_scatter x1, waiting for transfers between devices, local(): lax.psum_scatter(dense, 'expert', scatter_dimension=0, tiled=True)  4.9 us
    dot_general x1, matrix products, local(): jnp.dot(gradient, lax.all_gather(grad_factor[0], 'dp', axis=1, tiled=True...  3.16 us
    reduce_sum x1, other arithmetic, local(): jnp.sum(jnp.square(activ.astype(jnp.float32)), 1)  3.07 us
    dot_general x1, matrix products, local(): lax.dot_general(onehot, scores, contract, precision=lax.Precision.HIGHEST)  2.36 us
  transfers between devices with their start and end apart: 3, of which 3 were waited for; matrix products, arithmetic and copies ran while one was open for 10% of the time, Pallas kernels for 0%

commit v1 on v0

v1 whole, which is shorter than its diff:
```python
import functools

import jax
import jax.numpy as jnp
from jax import lax
from jax.experimental import pallas as pl
from jax.experimental.pallas import tpu as pltpu
from jax.sharding import PartitionSpec as P

RANK = 32
TOK_DEV = 256
LANES = 128
PACK = 16
V_PIECES = 2

epsilon = 1e-06
MESH = pl.DeviceIdType.MESH
CONTRACT_LAST = (((1,), (1,)), ((), ()))


def round_up(value, unit):
    return -(-value // unit) * unit


def kernel(
    dims,
    count_ref,
    token_ref,
    acts_hbm,
    grads_hbm,
    gfac_hbm,
    vfac_hbm,
    out_ref,
    acts,
    grads,
    gfac,
    vfac,
    gproj,
    aproj,
    scores,
    onehot,
    dense,
    landed,
    load_sem,
    send_sem,
    recv_sem,
    zsend_sem,
    zrecv_sem,
):
    n_dp, n_exp, across, queries, real_cols = dims
    chips = n_dp // 2
    half = chips // 2
    rows, model = acts.shape
    cols = gfac.shape[2]
    me_e = lax.axis_index("expert")
    me = lax.axis_index("dp")
    core = me % 2
    other = 1 - core

    def walk(index):
        line, at = index // across, index % across
        back = line % 2
        return line * across + at + back * (across - 1 - 2 * at)

    place = walk(me // 2)

    def chip_at(step):
        return walk((place + step + chips) % chips)

    mine = chip_at(0)
    ahead = chip_at(1) * 2 + core
    behind = chip_at(-1) * 2 + core
    partner = mine * 2 + other

    width = model // V_PIECES
    pieces = [None] + [pl.ds(i * width, width) for i in range(V_PIECES)]

    def held(chip, side, piece):
        if pieces[piece] is None:
            return gfac.at[chip, side]
        return vfac.at[chip, side, :, pieces[piece]]

    def own(piece):
        if pieces[piece] is None:
            return gfac_hbm
        return vfac_hbm.at[:, pieces[piece]]

    sent = []

    def send(src, chip, side, piece, target):
        copy = pltpu.make_async_remote_copy(
            src_ref=src,
            dst_ref=held(chip, side, piece),
            send_sem=send_sem.at[len(sent)],
            recv_sem=recv_sem.at[chip, side, piece],
            device_id=(me_e, target),
            device_id_type=MESH,
        )
        copy.start()
        sent.append(copy)

    def arrived(chip, side, piece):
        pltpu.make_async_remote_copy(
            src_ref=held(chip, side, piece),
            dst_ref=held(chip, side, piece),
            send_sem=send_sem.at[0],
            recv_sem=recv_sem.at[chip, side, piece],
            device_id=(me_e, partner),
            device_id_type=MESH,
        ).wait_recv()

    loads = [
        pltpu.make_async_copy(own(j), held(mine, core, j), load_sem.at[j])
        for j in range(len(pieces))
    ]
    load_grads = pltpu.make_async_copy(grads_hbm, grads, load_sem.at[len(pieces)])
    load_acts = pltpu.make_async_copy(acts_hbm, acts, load_sem.at[len(pieces) + 1])

    barrier = pltpu.get_barrier_semaphore()
    for target in (ahead, behind, partner):
        pl.semaphore_signal(barrier, inc=1, device_id=(me_e, target), device_id_type=MESH)
    for i in range(1, n_exp):
        pl.semaphore_signal(
            barrier, inc=1, device_id=((me_e + i) % n_exp, me), device_id_type=MESH
        )
    for copy in loads:
        copy.start()
    load_grads.start()
    load_acts.start()
    pl.semaphore_wait(barrier, 3 + n_exp - 1)

    for j in range(len(pieces)):
        send(own(j), mine, core, j, ahead)
        send(own(j), mine, core, j, behind)
        send(own(j), mine, core, j, partner)

    token_ids = lax.broadcasted_iota(jnp.int32, onehot.shape, 0)
    slot_ids = lax.broadcasted_iota(jnp.int32, (1, rows), 1)
    names = jnp.where(slot_ids < count_ref[0, 0], token_ref[...], -1)
    onehot[...] = (token_ids == names).astype(jnp.float32).astype(onehot.dtype)
    load_grads.wait()
    load_acts.wait()

    def energy(ref):
        total = jnp.zeros((rows, LANES), jnp.float32)
        for i in range(ref.shape[1] // LANES):
            part = ref[:, i * LANES : (i + 1) * LANES].astype(jnp.float32)
            total = total + part * part
        return jnp.sum(total, axis=1, keepdims=True)

    lane_ids = lax.broadcasted_iota(jnp.int32, (rows, LANES), 1)
    scores[...] = jnp.where(lane_ids == queries, energy(acts) * energy(grads), 0.0)

    def project(chip, piece, buf):
        if pieces[piece] is None:
            factor = gfac[chip].reshape(2 * cols, gfac.shape[3])
            gproj[buf] = lax.dot_general(
                grads[...], factor, CONTRACT_LAST, preferred_element_type=jnp.float32
            )
            return
        factor = vfac[chip, :, :, pieces[piece]].reshape(2 * cols, width)
        part = lax.dot_general(
            acts[:, pieces[piece]], factor, CONTRACT_LAST, preferred_element_type=jnp.float32
        )
        if piece == 1:
            aproj[buf] = part
        else:
            aproj[buf] += part

    def score(chip, buf):
        local_ids = lax.broadcasted_iota(jnp.int32, (2 * cols, LANES), 0)
        query_ids = lax.broadcasted_iota(jnp.int32, (2 * cols, LANES), 1)
        second = (local_ids >= cols).astype(jnp.int32)
        column = (2 * chip + second) * real_cols + local_ids - second * cols
        low = query_ids * RANK
        grouping = (column >= low) & (column < low + RANK) & (query_ids < queries)
        grouping = grouping.astype(jnp.float32).astype(jnp.bfloat16)
        product = aproj[buf] * gproj[buf]
        high = product.astype(jnp.bfloat16)
        rest = (product - high.astype(jnp.float32)).astype(jnp.bfloat16)
        scores[...] += jnp.dot(
            high, grouping, preferred_element_type=jnp.float32
        ) + jnp.dot(rest, grouping, preferred_element_type=jnp.float32)

    for j in range(len(pieces)):
        loads[j].wait()
        arrived(mine, other, j)
        project(mine, j, 0)
    score(mine, 0)

    for step in range(1, half + 1):
        last = step == half
        sources = [chip_at(-step)] if last else [chip_at(-step), chip_at(step)]
        for j in range(len(pieces) + 1):
            if j < len(pieces):
                for chip in sources:
                    arrived(chip, core, j)
                    send(held(chip, core, j), chip, core, j, partner)
                if step < half - 1:
                    send(held(sources[0], core, j), sources[0], core, j, ahead)
                    send(held(sources[1], core, j), sources[1], core, j, behind)
                elif step == half - 1:
                    chip = chip_at(step * (2 * core - 1))
                    target = chip_at(1 - 2 * core) * 2 + core
                    send(held(chip, core, j), chip, core, j, target)
            if j > 0:
                for buf, chip in enumerate(sources):
                    arrived(chip, other, j - 1)
                    project(chip, j - 1, buf)
        for buf, chip in enumerate(sources):
            score(chip, buf)

    total = scores[...]
    high = total.astype(jnp.bfloat16)
    rest = (total - high.astype(jnp.float32)).astype(jnp.bfloat16)
    summed = jnp.dot(
        onehot[...],
        jnp.concatenate([high, rest], axis=1),
        preferred_element_type=jnp.float32,
    )
    turned = (summed[:, :LANES] + summed[:, LANES:]).T[: dense.shape[1]]
    for i in range(n_exp):
        dense[i] = turned[:, i * TOK_DEV : (i + 1) * TOK_DEV]
    zcopies = []
    for i in range(1, n_exp):
        target = (me_e + i) % n_exp
        copy = pltpu.make_async_remote_copy(
            src_ref=dense.at[target],
            dst_ref=landed.at[i - 1],
            send_sem=zsend_sem.at[i - 1],
            recv_sem=zrecv_sem.at[i - 1],
            device_id=(target, me),
            device_id_type=MESH,
        )
        copy.start()
        zcopies.append(copy)
    result = dense[me_e]
    for i, copy in enumerate(zcopies):
        copy.wait_recv()
        result = result + landed[i]
    out_ref[...] = result
    for copy in zcopies:
        copy.wait_send()
    for copy in sent:
        copy.wait_send()


def local(dims, row_acts, row_grads, grad_factor, value_factor, counts, row_token):
    n_dp, n_exp, across, queries, real_cols = dims
    gfac, vfac = grad_factor[0].T, value_factor[0].T
    cols = round_up(real_cols, PACK)
    if cols != real_cols:
        pad = ((0, cols - real_cols), (0, 0))
        gfac, vfac = jnp.pad(gfac, pad), jnp.pad(vfac, pad)
    rows, model = row_acts.shape[1:]
    units = row_grads.shape[2]
    chips = n_dp // 2
    depth = round_up(queries + 1, 8)
    n_pieces = 1 + V_PIECES
    bufs = 2
    n_sends = n_pieces * (3 + sum(
        (1 if s == chips // 2 else 3 if s == chips // 2 - 1 else 4)
        for s in range(1, chips // 2 + 1)
    ))
    any_space = pl.BlockSpec(memory_space=pl.ANY)
    sums = pl.pallas_call(
        functools.partial(kernel, dims),
        name="influence_exchange",
        out_shape=jax.ShapeDtypeStruct((depth, TOK_DEV), jnp.float32),
        in_specs=[
            pl.BlockSpec(memory_space=pltpu.SMEM),
            pl.BlockSpec(memory_space=pltpu.VMEM),
            any_space,
            any_space,
            any_space,
            any_space,
        ],
        out_specs=pl.BlockSpec(memory_space=pltpu.VMEM),
        scratch_shapes=[
            pltpu.VMEM((rows, model), jnp.bfloat16),
            pltpu.VMEM((rows, units), jnp.bfloat16),
            pltpu.VMEM((chips, 2, cols, units), jnp.bfloat16),
            pltpu.VMEM((chips, 2, cols, model), jnp.bfloat16),
            pltpu.VMEM((bufs, rows, 2 * cols), jnp.float32),
            pltpu.VMEM((bufs, rows, 2 * cols), jnp.float32),
            pltpu.VMEM((rows, LANES), jnp.float32),
            pltpu.VMEM((n_exp * TOK_DEV, rows), jnp.bfloat16),
            pltpu.VMEM((n_exp, depth, TOK_DEV), jnp.float32),
            pltpu.VMEM((n_exp - 1, depth, TOK_DEV), jnp.float32),
            pltpu.SemaphoreType.DMA((n_pieces + 2,)),
            pltpu.SemaphoreType.DMA((n_sends,)),
            pltpu.SemaphoreType.DMA((chips, 2, n_pieces)),
            pltpu.SemaphoreType.DMA((n_exp - 1,)),
            pltpu.SemaphoreType.DMA((n_exp - 1,)),
        ],
        compiler_params=pltpu.CompilerParams(
            collective_id=0, has_side_effects=True, vmem_limit_bytes=60 * 1024 * 1024
        ),
    )(counts, row_token, row_acts[0], row_grads[0], gfac, vfac)
    factor = lax.rsqrt(sums[queries] / (model * units) + epsilon) / jnp.sqrt(jnp.float32(RANK))
    return (sums[:queries] * factor[None, :]).T


def solution(mesh):
    n_exp, n_dp = mesh.shape["expert"], mesh.shape["dp"]
    across = len({d.coords[0] for d in mesh.devices.flat})

    def whole(row_acts, row_grads, grad_factor, value_factor, counts, row_token):
        all_cols = grad_factor.shape[2]
        dims = (n_dp, n_exp, across, all_cols // RANK, all_cols // n_dp)
        return jax.shard_map(
            functools.partial(local, dims),
            mesh=mesh,
            in_specs=(
                P("expert", "dp", None),
                P("expert", "dp", None),
                P("expert", None, "dp"),
                P("expert", None, "dp"),
                P("expert", "dp"),
                P("expert", "dp"),
            ),
            out_specs=P(("expert", "dp"), None),
            check_vma=False,
        )(row_acts, row_grads, grad_factor, value_factor, counts, row_token)

    return whole
```

time: 108 us -> 40.2 us (0.37)
  waiting for transfers between devices: 59.5 us -> 0 us
  Pallas kernels: 0 us -> 37.2 us
  matrix products: 15.1 us -> 0 us
  between operations: 14.5 us -> 0.66 us
  blocking collectives: 11.7 us -> 0 us
  other arithmetic: 6.31 us -> 2.06 us
    all_gather x2 -> x0, waiting for transfers between devices: 53.2 us -> none  [the longest x1 30.9 us: local(): lax.all_gather(value_factor[0], 'dp', axis=1, tiled=True)]
    pallas_call x0 -> x1, Pallas kernels: none -> 37.2 us  [local(): pl.pallas_call(functools.partial(kernel, dims), name='influence_exchange'...]
    dot_general x5 -> x0, matrix products: 15.1 us -> none  [the longest x1 6.22 us: local(): jnp.dot(activ, lax.all_gather(value_factor[0], 'dp', axis=1, tiled=True),...]
    unnamed x1 -> x0, blocking collectives: 11.7 us -> none
    reduce_scatter x1 -> x0, waiting for transfers between devices: 4.9 us -> none  [local(): lax.psum_scatter(dense, 'expert', scatter_dimension=0, tiled=True)]
    reduce_sum x2 -> x0, other arithmetic: 4.86 us -> none  [the longest x1 3.07 us: local(): jnp.sum(jnp.square(activ.astype(jnp.float32)), 1)]
    unnamed x3 -> x0, waiting for transfers between devices: 1.42 us -> none
    mul x2 -> x0, other arithmetic: 1.35 us -> none  [the longest x1 1.35 us: local(): return totals * factor[:, None]]
  transfers between devices with their start and end apart: 3 -> 0, of which waited for: 3 -> 0; matrix products, arithmetic and copies ran while one was open for 10% -> 0% of each run, Pallas kernels for 0% -> 0%
where the time goes in v1:
time: 40.2 us; the launch traced here: 39.9 us
  Pallas kernels  37.2 us (93%)
  other arithmetic  2.06 us (5%)
  between operations  0.66 us (2%)
    pallas_call x1, Pallas kernels, local(): pl.pallas_call(functools.partial(kernel, dims), name='influence_exchange'...  37.2 us
    transpose x1, other arithmetic, local(): return (sums[:queries] * factor[None, :]).T  1.35 us

profile of v1, /device:TPU:0, one launch (start us, length us, event | category | flops | bytes accessed | tf_op | source)
XLA Modules:
  0.0 39.9 jit_solution(572841046247268498)
XLA Ops:
  0.7 37.2 %influence_exchange.1 = f32[32,256]{1,0:T(8,128)} custom-call(s32[1,1]{1,0:T(1,128)S(6)} %copy.7.count_ref, s32[1,1024]{1,0:T(1,128)} %token_ref.1, bf16[1024,2048]{1,0:T(8,128)(2,1)} %bitcast.11, bf16[1024,768]{1,0:T(8,128)(2,1)} %bitcast.12, bf16[96,768]{1,0:T(8,128)(2,1)} %bitcast.14, bf16[96,2048]{1,0:T(8,128)(2,1)} %bitcast.13), custom_call_target="tpu_custom_call" | custom-call | tf_op jit(solution)/shard_map/influence_exchange/pallas_call | solution.py:266
  37.9 0.7 %rsqrt_multiply_fusion = f32[1,256]{1,0:T(1,128)S(1)} fusion(f32[32,256]{1,0:T(8,128)} %influence_exchange.1), kind=kLoop, calls=%fused_computation.1 | loop fusion | flops 768 | bytes 2048 | tf_op jit(solution)/shard_map/div | solution.py:300
  38.6 1.4 %multiply_bitcast_fusion = f32[256,24]{0,1:T(8,128)} fusion(f32[32,256]{1,0:T(8,128)} %influence_exchange.1, f32[256]{0:T(256)S(1)} %bitcast.15), kind=kLoop, calls=%fused_computation | loop fusion | flops 6144 | bytes 50176 | tf_op jit(solution)/shard_map/transpose | solution.py:301

commit v2 on v1

--- a/solution.py
+++ b/solution.py
@@ -11,7 +11,7 @@
 TOK_DEV = 256
 LANES = 128
 PACK = 16
-V_PIECES = 2
+V_PARTS = (2, 4, 4)
 
 epsilon = 1e-06
 MESH = pl.DeviceIdType.MESH
@@ -41,6 +41,8 @@
     onehot,
     dense,
     landed,
+    far_dense,
+    far_landed,
     load_sem,
     send_sem,
     recv_sem,
@@ -72,8 +74,10 @@
     behind = chip_at(-1) * 2 + core
     partner = mine * 2 + other
 
-    width = model // V_PIECES
-    pieces = [None] + [pl.ds(i * width, width) for i in range(V_PIECES)]
+    pieces, start = [None], 0
+    for part in V_PARTS:
+        pieces.append(pl.ds(start, model // part))
+        start += model // part
 
     def held(chip, side, piece):
         if pieces[piece] is None:
@@ -151,97 +155,135 @@
     lane_ids = lax.broadcasted_iota(jnp.int32, (rows, LANES), 1)
     scores[...] = jnp.where(lane_ids == queries, energy(acts) * energy(grads), 0.0)
 
-    def project(chip, piece, buf):
-        if pieces[piece] is None:
-            factor = gfac[chip].reshape(2 * cols, gfac.shape[3])
-            gproj[buf] = lax.dot_general(
-                grads[...], factor, CONTRACT_LAST, preferred_element_type=jnp.float32
-            )
-            return
-        factor = vfac[chip, :, :, pieces[piece]].reshape(2 * cols, width)
-        part = lax.dot_general(
-            acts[:, pieces[piece]], factor, CONTRACT_LAST, preferred_element_type=jnp.float32
-        )
-        if piece == 1:
-            aproj[buf] = part
-        else:
-            aproj[buf] += part
-
-    def score(chip, buf):
+    def project_grads(chip, buf):
+        factor = gfac[chip].reshape(2 * cols, gfac.shape[3])
+        gproj[buf] = lax.dot_general(
+            grads[...], factor, CONTRACT_LAST, preferred_element_type=jnp.float32
+        )
+
+    def project_acts(chip, span):
+        factor = vfac[chip, :, :, span].reshape(2 * cols, span.size)
+        return lax.dot_general(
+            acts[:, span], factor, CONTRACT_LAST, preferred_element_type=jnp.float32
+        )
+
+    def split(value):
+        high = value.astype(jnp.bfloat16)
+        return high, (value - high.astype(jnp.float32)).astype(jnp.bfloat16)
+
+    def score(chip, product, first):
         local_ids = lax.broadcasted_iota(jnp.int32, (2 * cols, LANES), 0)
-        query_ids = lax.broadcasted_iota(jnp.int32, (2 * cols, LANES), 1)
+        query_ids = lax.broadcasted_iota(jnp.int32, (2 * cols, LANES), 1) + first
         second = (local_ids >= cols).astype(jnp.int32)
         column = (2 * chip + second) * real_cols + local_ids - second * cols
         low = query_ids * RANK
         grouping = (column >= low) & (column < low + RANK) & (query_ids < queries)
         grouping = grouping.astype(jnp.float32).astype(jnp.bfloat16)
-        product = aproj[buf] * gproj[buf]
-        high = product.astype(jnp.bfloat16)
-        rest = (product - high.astype(jnp.float32)).astype(jnp.bfloat16)
-        scores[...] += jnp.dot(
-            high, grouping, preferred_element_type=jnp.float32
-        ) + jnp.dot(rest, grouping, preferred_element_type=jnp.float32)
+        high, rest = split(product)
+        return jnp.dot(high, grouping, preferred_element_type=jnp.float32) + jnp.dot(
+            rest, grouping, preferred_element_type=jnp.float32
+        )
+
+    def hand_over(total, stage, own_sums, others):
+        summed = jnp.dot(
+            onehot[...],
+            jnp.concatenate(split(total), axis=1),
+            preferred_element_type=jnp.float32,
+        )
+        turned = (summed[:, :LANES] + summed[:, LANES:]).T[: own_sums.shape[1]]
+        for i in range(n_exp):
+            own_sums[i] = turned[:, i * TOK_DEV : (i + 1) * TOK_DEV]
+        copies = []
+        for i in range(1, n_exp):
+            target = (me_e + i) % n_exp
+            copy = pltpu.make_async_remote_copy(
+                src_ref=own_sums.at[target],
+                dst_ref=others.at[i - 1],
+                send_sem=zsend_sem.at[stage, i - 1],
+                recv_sem=zrecv_sem.at[stage, i - 1],
+                device_id=(target, me),
+                device_id_type=MESH,
+            )
+            copy.start()
+            copies.append(copy)
+        return copies
+
+    def collect(copies, own_sums, others):
+        result = own_sums[me_e]
+        for i, copy in enumerate(copies):
+            copy.wait_recv()
+            result = result + others[i]
+        return result
 
     for j in range(len(pieces)):
         loads[j].wait()
         arrived(mine, other, j)
-        project(mine, j, 0)
-    score(mine, 0)
-
-    for step in range(1, half + 1):
-        last = step == half
-        sources = [chip_at(-step)] if last else [chip_at(-step), chip_at(step)]
-        for j in range(len(pieces) + 1):
-            if j < len(pieces):
-                for chip in sources:
-                    arrived(chip, core, j)
-                    send(held(chip, core, j), chip, core, j, partner)
-                if step < half - 1:
-                    send(held(sources[0], core, j), sources[0], core, j, ahead)
-                    send(held(sources[1], core, j), sources[1], core, j, behind)
-                elif step == half - 1:
-                    chip = chip_at(step * (2 * core - 1))
-                    target = chip_at(1 - 2 * core) * 2 + core
-                    send(held(chip, core, j), chip, core, j, target)
-            if j > 0:
-                for buf, chip in enumerate(sources):
-                    arrived(chip, other, j - 1)
-                    project(chip, j - 1, buf)
-        for buf, chip in enumerate(sources):
-            score(chip, buf)
-
-    total = scores[...]
-    high = total.astype(jnp.bfloat16)
-    rest = (total - high.astype(jnp.float32)).astype(jnp.bfloat16)
-    summed = jnp.dot(
-        onehot[...],
-        jnp.concatenate([high, rest], axis=1),
-        preferred_element_type=jnp.float32,
-    )
-    turned = (summed[:, :LANES] + summed[:, LANES:]).T[: dense.shape[1]]
-    for i in range(n_exp):
-        dense[i] = turned[:, i * TOK_DEV : (i + 1) * TOK_DEV]
-    zcopies = []
-    for i in range(1, n_exp):
-        target = (me_e + i) % n_exp
-        copy = pltpu.make_async_remote_copy(
-            src_ref=dense.at[target],
-            dst_ref=landed.at[i - 1],
-            send_sem=zsend_sem.at[i - 1],
-            recv_sem=zrecv_sem.at[i - 1],
-            device_id=(target, me),
-            device_id_type=MESH,
-        )
-        copy.start()
-        zcopies.append(copy)
-    result = dense[me_e]
-    for i, copy in enumerate(zcopies):
-        copy.wait_recv()
-        result = result + landed[i]
-    out_ref[...] = result
-    for copy in zcopies:
-        copy.wait_send()
-    for copy in sent:
+        if j == 0:
+            project_grads(mine, 0)
+    aproj[0] = project_acts(mine, pl.ds(0, model))
+    scores[...] += score(mine, aproj[0] * gproj[0], 0)
+
+    def sources_of(step):
+        return [chip_at(-step)] if step == half else [chip_at(-step), chip_at(step)]
+
+    def pass_on(step, j):
+        sources = sources_of(step)
+        for chip in sources:
+            arrived(chip, core, j)
+            send(held(chip, core, j), chip, core, j, partner)
+        if step < half - 1:
+            send(held(sources[0], core, j), sources[0], core, j, ahead)
+            send(held(sources[1], core, j), sources[1], core, j, behind)
+        elif step == half - 1:
+            chip = chip_at(step * (2 * core - 1))
+            target = chip_at(1 - 2 * core) * 2 + core
+            send(held(chip, core, j), chip, core, j, target)
+
+    far_chip = chip_at(half)
+    base = 2 * far_chip * real_cols // RANK
+
+    def multiply(step, j):
+        far_scores = None
+        for buf, chip in enumerate(sources_of(step)):
+            arrived(chip, other, j)
+            if j == 0:
+                project_grads(chip, buf)
+            elif j == 1:
+                aproj[buf] = project_acts(chip, pieces[j])
+            elif j < len(pieces) - 1:
+                aproj[buf] += project_acts(chip, pieces[j])
+            else:
+                product = (aproj[buf] + project_acts(chip, pieces[j])) * gproj[buf]
+                if step == half:
+                    far_scores = score(chip, product, base)
+                else:
+                    scores[...] += score(chip, product, 0)
+        return far_scores
+
+    order = [(step, j) for step in range(1, half + 1) for j in range(len(pieces))]
+    done, near = 0, None
+    for at, (step, j) in enumerate(order):
+        pass_on(step, j)
+        if step == half and j == 1:
+            near = hand_over(scores[...], 0, dense, landed)
+        lag = 1 if order[done][0] < half else 2
+        if at - done >= lag:
+            multiply(*order[done])
+            done += 1
+    for event in order[done:]:
+        far_scores = multiply(*event)
+
+    far = hand_over(far_scores, 1, far_dense, far_landed)
+    result = collect(near, dense, landed)
+    late = collect(far, far_dense, far_landed)
+    row_ids = lax.broadcasted_iota(jnp.int32, result.shape, 0)
+    for i in range(late.shape[0]):
+        result = result + jnp.where(row_ids == base + i, late[i : i + 1], 0.0)
+    energy_sum = result[queries : queries + 1]
+    factor = lax.rsqrt(energy_sum / (model * grads.shape[1]) + epsilon)
+    factor = factor / jnp.sqrt(jnp.float32(RANK))
+    out_ref[...] = result[:queries] * factor
+    for copy in near + far + sent:
         copy.wait_send()
 
 
@@ -256,17 +298,18 @@
     units = row_grads.shape[2]
     chips = n_dp // 2
     depth = round_up(queries + 1, 8)
-    n_pieces = 1 + V_PIECES
+    n_pieces = 1 + len(V_PARTS)
+    few = round_up((2 * real_cols - 1) // RANK + 2, 8)
     bufs = 2
     n_sends = n_pieces * (3 + sum(
         (1 if s == chips // 2 else 3 if s == chips // 2 - 1 else 4)
         for s in range(1, chips // 2 + 1)
     ))
     any_space = pl.BlockSpec(memory_space=pl.ANY)
-    sums = pl.pallas_call(
+    turned = pl.pallas_call(
         functools.partial(kernel, dims),
         name="influence_exchange",
-        out_shape=jax.ShapeDtypeStruct((depth, TOK_DEV), jnp.float32),
+        out_shape=jax.ShapeDtypeStruct((queries, TOK_DEV), jnp.float32),
         in_specs=[
             pl.BlockSpec(memory_space=pltpu.SMEM),
             pl.BlockSpec(memory_space=pltpu.VMEM),
@@ -287,18 +330,19 @@
             pltpu.VMEM((n_exp * TOK_DEV, rows), jnp.bfloat16),
             pltpu.VMEM((n_exp, depth, TOK_DEV), jnp.float32),
             pltpu.VMEM((n_exp - 1, depth, TOK_DEV), jnp.float32),
+            pltpu.VMEM((n_exp, few, TOK_DEV), jnp.float32),
+            pltpu.VMEM((n_exp - 1, few, TOK_DEV), jnp.float32),
             pltpu.SemaphoreType.DMA((n_pieces + 2,)),
             pltpu.SemaphoreType.DMA((n_sends,)),
             pltpu.SemaphoreType.DMA((chips, 2, n_pieces)),
-            pltpu.SemaphoreType.DMA((n_exp - 1,)),
-            pltpu.SemaphoreType.DMA((n_exp - 1,)),
+            pltpu.SemaphoreType.DMA((2, n_exp - 1)),
+            pltpu.SemaphoreType.DMA((2, n_exp - 1)),
         ],
         compiler_params=pltpu.CompilerParams(
             collective_id=0, has_side_effects=True, vmem_limit_bytes=60 * 1024 * 1024
         ),
     )(counts, row_token, row_acts[0], row_grads[0], gfac, vfac)
-    factor = lax.rsqrt(sums[queries] / (model * units) + epsilon) / jnp.sqrt(jnp.float32(RANK))
-    return (sums[:queries] * factor[None, :]).T
+    return turned.T
 
 
 def solution(mesh):

time: 40.2 us -> 37.8 us (0.940)
  other arithmetic: 2.06 us -> 0 us
  Pallas kernels: 37.2 us -> 35.6 us
  local copies, waits for them, and re-layouts: 0 us -> 1.35 us
    pallas_call x1, Pallas kernels: 37.2 us -> 35.6 us  [local(): pl.pallas_call(functools.partial(kernel, dims), name='influence_exchange'...]
    transpose x1 -> x0, other arithmetic: 1.35 us -> none  [local(): return (sums[:queries] * factor[None, :]).T]
    unnamed x0 -> x1, local copies, waits for them, and re-layouts: none -> 1.35 us
    div x1 -> x0, other arithmetic: 0.7 us -> none  [local(): lax.rsqrt(sums[queries] / (model * units) + epsilon)]
where the time goes in v2:
time: 37.8 us; the launch traced here: 37.6 us
  Pallas kernels  35.6 us (94%)
  local copies, waits for them, and re-layouts  1.35 us (4%)
  between operations  0.66 us (2%)
    pallas_call x1, Pallas kernels, local(): pl.pallas_call(functools.partial(kernel, dims), name='influence_exchange'...  35.6 us
    unnamed x1, local copies, waits for them, and re-layouts  1.35 us

profile of v2, /device:TPU:0, one launch (start us, length us, event | category | flops | bytes accessed | tf_op | source)
XLA Modules:
  0.0 37.6 jit_solution(9472825934804465147)
XLA Ops:
  0.7 35.6 %influence_exchange.1 = f32[24,256]{1,0:T(8,128)} custom-call(s32[1,1]{1,0:T(1,128)S(6)} %copy.8.count_ref, s32[1,1024]{1,0:T(1,128)} %token_ref.1, bf16[1024,2048]{1,0:T(8,128)(2,1)} %bitcast.9, bf16[1024,768]{1,0:T(8,128)(2,1)} %bitcast.10, bf16[96,768]{1,0:T(8,128)(2,1)} %bitcast.12, bf16[96,2048]{1,0:T(8,128)(2,1)} %bitcast.11), custom_call_target="tpu_custom_call" | custom-call | tf_op jit(solution)/shard_map/influence_exchange/pallas_call | solution.py:309
  36.2 1.3 %copy.9 = f32[256,24]{0,1:T(8,128)} copy(f32[256,24]{0,1:T(8,128)} %bitcast.13) | data formatting | bytes 49152
